TPU v7x, 32 devices: a whole 2x2x4 slice. The times are simulated.
32 devices in a mesh: groups: 2 (over x), seq: 16 (over z, y, core).
Axes of the slice: x: 2, y: 2, z: 4, core: 2. Of those that a mesh axis runs over, the one named last changes fastest.
Arguments:
- latent: bfloat16 [32, 32768], P(('groups', 'seq')), parts along dimension 0, may hold values from -6 to 6
- text_embed: bfloat16 [4, 128, 3072], P('groups'), parts along dimension 0, may hold values from -6 to 6
- text_mask: int32 [4, 128], P('groups'), parts along dimension 0, may hold values from 0 to 1, as said below
- modulation: float32 [4, 5, 3072], P('groups'), parts along dimension 0, may hold values from -3 to 10
- w_in: bfloat16 [64, 3072], replicated, may hold values from -0.75 to 0.75
- w_qkv: bfloat16 [3072, 4608], P(None, 'seq'), may hold values from -0.109375 to 0.109375
- w_attn_out: bfloat16 [1536, 3072], P(None, 'seq'), may hold values from -0.15625 to 0.15625
- w_final: bfloat16 [3072, 64], replicated, may hold values from -0.109375 to 0.109375
Outputs:
- guided: float32 [32, 32768], P(('groups', 'seq')), parts along dimension 0
There are 2 independent parts, one for each index of `groups`. A program takes and returns all parts, laid end to end along the dimension named above; an argument that names none is the same for every part. Nothing has to cross between parts.
Inputs may be any that keep to these rules, and one draw needn't show every extreme that they name: `text_mask`: each row is 1 on a leading run of 1 to 127 positions and 0 after it.
All inputs are finite; a program needn't handle non-finite values.
Results may differ from a plain program's by a relative error of at most 0.007.
The roundings to bfloat16 on the way count: a program that leaves them out, or rounds other values in their place, can miss the bound.
Values may be sent and summed in bfloat16 or wider, within the bound.
A program may use at most 128 MiB of HBM per device.

v0:
```python
import functools

import jax
import jax.numpy as jnp
from jax import lax
from jax.experimental import pallas as pl
from jax.experimental.pallas import tpu as pltpu
from jax.sharding import PartitionSpec as P

HDIM = 128
SHEADS = 6
THEADS = 6
CHAN = 64
HEADS = 12
ROLES = 4
SROLES = 2

EPS = 1e-06
GUIDE = 5.0
NT = (((1,), (1,)), ((), ()))


def dot_nt(a, b):
    return lax.dot_general(a, b, NT, preferred_element_type=jnp.float32)


def normalize(values):
    center = values - jnp.mean(values, axis=-1, keepdims=True)
    spread = jnp.mean(center * center, axis=-1, keepdims=True)
    return center * lax.rsqrt(spread + EPS)


def block_kernel(
    count, gran, lat, text, mask, mods, w_in, wq, wo, wf, out,
    latbuf, wbuf, hbuf, tbuf, pbuf, obuf, wob, jbuf, blk, acc, predb,
    lat_send, lat_recv, w_send, w_xsend, w_tsend, w_recv, wo_send, wo_xsend, wo_tsend, wo_recv,
    j_send, j_recv, p_send, p_recv, loc,
):
    positions = lat.shape[0]
    depth = w_in.shape[1]
    n2 = count // 2
    chips = n2 // 2
    team, me = lax.axis_index("groups"), lax.axis_index("seq")
    plane = lax.rem(team, 2)
    half = lax.div(me, n2)
    local = lax.rem(me, n2)
    core = lax.rem(me, 2)
    chip = lax.div(local, 2)
    role = lax.rem(chip, ROLES)
    members = n2 // ROLES
    pairs = members // 2
    spot = lax.div(chip, ROLES) * 2 + core
    span = positions // members
    rows = ROLES * positions
    width = wbuf.shape[1]
    offs = width // gran
    per_part = ROLES * offs
    mine = wq.shape[0] // gran
    is_spatial = role < SROLES

    twin = {"seq": me + 1 - 2 * core}
    across = {"groups": team + 1 - 2 * plane}

    def device(side, which, at):
        return side * n2 + (lax.div(at, 2) * ROLES + which) * 2 + lax.rem(at, 2)

    def remote(src, dst, send, recv, peer):
        return pltpu.make_async_remote_copy(
            src_ref=src, dst_ref=dst, send_sem=send, recv_sem=recv,
            device_id=peer, device_id_type=pl.DeviceIdType.MESH,
        )

    finish = []

    def go(src, dst, send, recv, peer):
        remote(src, dst, send, recv, peer).start()
        finish.append(lambda: remote(src, dst, send, recv, peer).wait_send())

    def push(src, dst, send, recv, to):
        def far():
            return remote(src, dst, send, recv, {"seq": to})

        @pl.when(to == me)
        def _():
            pltpu.make_async_copy(src, dst, recv).start()

        @pl.when(to != me)
        def _():
            far().start()

        def end():
            @pl.when(to != me)
            def _():
                far().wait_send()

        finish.append(end)

    def arrived(view, sem):
        pltpu.make_async_copy(view, view, sem).wait()

    def aligned(value, unit):
        return pl.multiple_of(value, unit)

    barrier = pltpu.get_barrier_semaphore()

    def greet(step, carry):
        peer = lax.rem(me + step, count)
        pl.semaphore_signal(barrier, inc=1, device_id={"seq": peer}, device_id_type=pl.DeviceIdType.MESH)
        return carry

    pl.semaphore_signal(barrier, inc=1, device_id=across, device_id_type=pl.DeviceIdType.MESH)
    lax.fori_loop(1, count, greet, 0)

    shard = wo.shape[0]
    unit = shard // 3
    own_wo = pltpu.make_async_copy(wo, wob.at[pl.ds(aligned(me * shard, shard), shard)], loc.at[0])
    own_text = pltpu.make_async_copy(text.at[half], tbuf, loc.at[1])
    own_wo.start()
    own_text.start()
    pl.semaphore_wait(barrier, count)

    for which in range(SROLES):
        to = device(half, which, lax.div(local, ROLES))
        slot = lax.rem(local, ROLES)
        push(
            lat, latbuf.at[pl.ds(aligned(slot * positions, positions), positions)],
            lat_send.at[which], lat_recv.at[slot], to,
        )
    for which in range(SROLES, ROLES):
        for at in range(members):
            push(
                lat.at[pl.ds(at * span, span)], latbuf.at[pl.ds(aligned(local * span, span), span)],
                lat_send.at[SROLES + (which - SROLES) * members + at], lat_recv.at[local],
                device(half, which, jnp.int32(at)),
            )

    def slot_view(part, off):
        return wbuf.at[part, pl.ds(aligned(off * gran, gran), gran)]

    def w_sem(part, off):
        return part * offs + off

    for far in (1, 0):
        for k in range(mine):
            number = me * mine + k
            part = lax.div(number, per_part)
            which = lax.div(lax.rem(number, per_part), offs)
            off = lax.rem(number, offs)
            side = half + far * (1 - 2 * half)
            for pair in range(pairs):
                to = side * n2 + (pair * ROLES + which) * 2 + lax.rem(off, 2)

                def send(k=k, part=part, off=off, to=to, far=far, pair=pair):
                    return (
                        wq.at[pl.ds(k * gran, gran)], slot_view(part, off),
                        w_send.at[k, far, pair], w_recv.at[w_sem(part, off)],
                    )

                turn = lax.rem(lax.div(off, 2), 2) == plane

                @pl.when(jnp.logical_and(turn, to == me))
                def _(send=send):
                    src, dst, _, recv = send()
                    pltpu.make_async_copy(src, dst, recv).start()

                @pl.when(jnp.logical_and(turn, to != me))
                def _(send=send, to=to):
                    remote(*send(), {"seq": to}).start()

                def end(send=send, to=to, turn=turn):
                    @pl.when(jnp.logical_and(turn, to != me))
                    def _():
                        remote(*send(), {"seq": to}).wait_send()

                finish.append(end)

    def wo_direct(owner):
        return pl.ds(aligned(owner * shard + plane * unit, unit), 2 * unit)

    def wo_cross(owner, side):
        return pl.ds(aligned(owner * shard + side * 2 * unit, unit), unit)

    mirror = me + n2 * (1 - 2 * half)
    own_direct = wo.at[pl.ds(aligned(plane * unit, unit), 2 * unit)]

    def in_half(step):
        return half * n2 + lax.rem(chip + step, chips) * 2 + core

    def in_other(step):
        return (1 - half) * n2 + lax.rem(chip + step, chips) * 2 + core

    go(own_direct, wob.at[wo_direct(me)], wo_send.at[0, 0], wo_recv.at[me, 0], {"seq": mirror})
    for step in range(1, chips):
        go(
            own_direct, wob.at[wo_direct(me)], wo_send.at[0, step], wo_recv.at[me, 0],
            {"seq": in_half(step)},
        )
    own_rows = wob.at[pl.ds(aligned(me * shard, shard), shard)]
    go(wo, own_rows, wo_tsend.at[0, 0], wo_recv.at[me, 0], twin)

    def wo_spread(owner, number):
        go(
            wob.at[wo_cross(owner, plane)], wob.at[wo_cross(owner, plane)],
            wo_xsend.at[number], wo_recv.at[owner, 1], across,
        )
        go(
            wob.at[wo_direct(owner)], wob.at[wo_direct(owner)],
            wo_tsend.at[1, number], wo_recv.at[owner, 0], twin,
        )

    def wo_take(owner, number):
        arrived(wob.at[wo_direct(owner)], wo_recv.at[owner, 0])
        wo_spread(owner, number)

    def wo_mirror():
        arrived(wob.at[wo_direct(mirror)], wo_recv.at[mirror, 0])
        for step in range(1, chips):
            go(
                wob.at[wo_direct(mirror)], wob.at[wo_direct(mirror)], wo_send.at[1, step],
                wo_recv.at[mirror, 0], {"seq": in_half(step)},
            )
        wo_spread(mirror, 0)

    def wo_others():
        return [(in_half(step), step) for step in range(1, chips)] + [
            (in_other(step), chips + step) for step in range(1, chips)
        ]

    def wo_cross_take():
        for owner, number in [(mirror, 0)] + wo_others():
            arrived(wob.at[wo_cross(owner, 1 - plane)], wo_recv.at[owner, 1])
            go(
                wob.at[wo_cross(owner, 1 - plane)], wob.at[wo_cross(owner, 1 - plane)],
                wo_tsend.at[2, number], wo_recv.at[owner, 1], twin,
            )

    def wo_wait():
        own_wo.wait()
        other = 1 - 2 * core
        arrived(wob.at[pl.ds(aligned((me + other) * shard, shard), shard)], wo_recv.at[me + other, 0])
        for owner, _ in [(mirror, 0)] + wo_others():
            arrived(wob.at[wo_direct(owner + other)], wo_recv.at[owner + other, 0])
            arrived(wob.at[wo_cross(owner + other, 1 - plane)], wo_recv.at[owner + other, 1])

    def mod(which):
        return jnp.where(half == 0, mods[which, 0:1, :], mods[which, 1:2, :])

    quarter = positions // 4

    def start_step(step, carry):
        at = pl.ds(aligned(step * quarter, quarter), quarter)
        blk[at, :] = jnp.dot(lat[at, :], w_in[...], preferred_element_type=jnp.float32)
        return carry

    lax.fori_loop(0, 4, start_step, 0)

    @pl.when(is_spatial)
    def _():
        for slot in range(ROLES):
            arrived(latbuf.at[pl.ds(slot * positions, positions)], lat_recv.at[slot])

    @pl.when(jnp.logical_not(is_spatial))
    def _():
        for frame in range(n2):
            arrived(latbuf.at[pl.ds(frame * span, span)], lat_recv.at[frame])

    tall = 128

    def hidden_step(step, carry):
        at = pl.ds(aligned(step * tall, tall), tall)
        begun = jnp.dot(latbuf[at, :], w_in[...], preferred_element_type=jnp.float32)
        hbuf[at, :] = (normalize(begun) * (1.0 + mod(1)) + mod(0)).astype(jnp.bfloat16)
        return carry

    lax.fori_loop(0, rows // tall, hidden_step, 0)
    own_text.wait()

    def order(step):
        return step + half * (2 - 2 * step)

    def first_take(step):
        part = order(step)
        for e in range(offs // 4):
            off = core + 2 * plane + 4 * e
            view, number = slot_view(part, off), w_sem(part, off)
            arrived(view, w_recv.at[number])
            go(view, view, w_xsend.at[number], w_recv.at[number], across)
            go(view, view, w_tsend.at[number], w_recv.at[number], twin)

    def second_take(step):
        part = order(step)
        for e in range(offs // 4):
            off = core + 2 * (1 - plane) + 4 * e
            view, number = slot_view(part, off), w_sem(part, off)
            arrived(view, w_recv.at[number])
            go(view, view, w_tsend.at[number], w_recv.at[number], twin)

    def third_take(step):
        part = order(step)
        for e in range(offs // 4):
            for side in range(2):
                off = 1 - core + 2 * side + 4 * e
                arrived(slot_view(part, off), w_recv.at[w_sem(part, off)])

    def project(step):
        part = order(step)

        def body(turn, carry):
            at = pl.ds(aligned(turn * positions, positions), positions)
            pbuf[part, at, :] = dot_nt(hbuf[at, :], wbuf[part]).astype(jnp.bfloat16)
            return carry

        lax.fori_loop(0, ROLES, body, 0)

        @pl.when(jnp.logical_and(is_spatial, part > 0))
        def _():
            pbuf[part, pl.ds(rows, tbuf.shape[0]), :] = dot_nt(tbuf[...], wbuf[part]).astype(jnp.bfloat16)

    first_take(0)
    first_take(1)
    second_take(0)
    third_take(0)
    project(0)
    first_take(2)
    second_take(1)
    third_take(1)
    wo_mirror()
    project(1)
    second_take(2)
    third_take(2)
    for owner, number in wo_others()[: chips - 1]:
        wo_take(owner, number)
    project(2)
    for owner, number in wo_others()[chips - 1 :]:
        wo_take(owner, number)

    scale = HDIM ** (-0.5)
    heads = width // HDIM
    words = tbuf.shape[0]
    lanes = pl.ds(aligned(role * width, width), width)

    def out_copy(src, dst, send, recv, to):
        return (src, dst, send, recv), to

    def spatial_send(frame):
        to = half * n2 + spot * ROLES + frame
        src = obuf.at[pl.ds(aligned(frame * positions, positions), positions)]
        return (src, jbuf.at[:, lanes], j_send.at[frame], j_recv.at[role]), to

    def temporal_send(frame):
        to = half * n2 + frame
        src = obuf.at[pl.ds(aligned(frame * span, span), span)]
        dst = jbuf.at[pl.ds(aligned(spot * span, span), span), lanes]
        recv = j_recv.at[SROLES + (role - SROLES) * members + spot]
        return (src, dst, j_send.at[frame], recv), to

    def dispatch(refs, to):
        src, dst, send, recv = refs

        @pl.when(to == me)
        def _():
            pltpu.make_async_copy(src, dst, recv).start()

        @pl.when(to != me)
        def _():
            remote(src, dst, send, recv, {"seq": to}).start()

    def drain(refs, to):
        @pl.when(to != me)
        def _():
            remote(*refs, {"seq": to}).wait_send()

    @pl.when(is_spatial)
    def _():
        live = jnp.where(half == 0, mask[0:1, :], mask[1:2, :]) > 0
        tallq = positions // 2

        def frame_step(frame, carry):
            base = frame * positions
            at = pl.ds(aligned(base, positions), positions)
            for head in range(heads):
                cols = pl.ds(head * HDIM, HDIM)
                keys, vals = pbuf[1, at, cols], pbuf[2, at, cols]
                tkeys, tvals = pbuf[1, pl.ds(rows, words), cols], pbuf[2, pl.ds(rows, words), cols]
                for piece in range(2):
                    here = pl.ds(aligned(base + piece * tallq, tallq), tallq)
                    query = pbuf[0, here, cols]
                    near = dot_nt(query, keys) * scale
                    side = jnp.where(live, dot_nt(query, tkeys) * scale, -1e30)
                    top = jnp.maximum(
                        jnp.max(near, axis=-1, keepdims=True), jnp.max(side, axis=-1, keepdims=True)
                    )
                    near = jnp.exp(near - top)
                    side = jnp.exp(side - top)
                    total = jnp.sum(near, axis=-1, keepdims=True) + jnp.sum(side, axis=-1, keepdims=True)
                    mixed = jnp.dot(
                        near.astype(jnp.bfloat16), vals, preferred_element_type=jnp.float32
                    ) + jnp.dot(side.astype(jnp.bfloat16), tvals, preferred_element_type=jnp.float32)
                    obuf[here, cols] = (mixed / total).astype(jnp.bfloat16)
            dispatch(*spatial_send(frame))
            return carry

        lax.fori_loop(0, ROLES, frame_step, 0)

    @pl.when(jnp.logical_not(is_spatial))
    def _():
        few = 256 // n2
        size = few * n2
        row_at = lax.rem(lax.broadcasted_iota(jnp.int32, (size, size), 0), few)
        col_at = lax.rem(lax.broadcasted_iota(jnp.int32, (size, size), 1), few)
        same = row_at == col_at

        def place_step(place, carry):
            def at(frame):
                return pl.ds(aligned(frame * span + place * few, few), few)

            for head in range(heads):
                cols = pl.ds(head * HDIM, HDIM)
                query, keys, vals = (
                    jnp.concatenate([pbuf[part, at(frame), cols] for frame in range(n2)], axis=0)
                    for part in range(3)
                )
                scores = jnp.where(same, dot_nt(query, keys) * scale, -1e30)
                weights = jnp.exp(scores - jnp.max(scores, axis=-1, keepdims=True))
                total = jnp.sum(weights, axis=-1, keepdims=True)
                mixed = jnp.dot(weights.astype(jnp.bfloat16), vals, preferred_element_type=jnp.float32)
                mixed = (mixed / total).astype(jnp.bfloat16)
                for frame in range(n2):
                    obuf[at(frame), cols] = mixed[frame * few : (frame + 1) * few]
            return carry

        lax.fori_loop(0, span // few, place_step, 0)

        def send_step(frame, carry):
            dispatch(*temporal_send(frame))
            return carry

        lax.fori_loop(0, n2, send_step, 0)

    wo_cross_take()
    wo_wait()
    for which in range(SROLES):
        arrived(jbuf.at[:, pl.ds(which * width, width)], j_recv.at[which])
    for which in range(SROLES, ROLES):
        for at in range(members):
            arrived(
                jbuf.at[pl.ds(at * span, span), pl.ds(which * width, width)],
                j_recv.at[SROLES + (which - SROLES) * members + at],
            )

    acc[...] = jnp.zeros_like(acc)
    strip = 512

    def mix_step(step, carry):
        cols = pl.ds(aligned(step * strip, strip), strip)
        gate = jnp.where(half == 0, mods[2, 0:1, cols], mods[2, 1:2, cols])
        value = blk[:, cols] + gate * dot_nt(jbuf[...], wob[cols, :])
        blk[:, cols] = value
        part = value[:, :128]
        for piece in range(1, strip // 128):
            part = part + value[:, piece * 128 : (piece + 1) * 128]
        acc[...] += part
        return carry

    lax.fori_loop(0, depth // strip, mix_step, 0)

    def swap(step):
        at = pl.ds(aligned(step * quarter, quarter), quarter)
        return remote(
            predb.at[0, at], predb.at[1, at], p_send.at[step], p_recv.at[step], {"seq": mirror}
        )

    def last_step(step, carry):
        at = pl.ds(aligned(step * quarter, quarter), quarter)
        mean = jnp.sum(acc[at, :], axis=-1, keepdims=True) / depth
        center = blk[at, :] - mean
        spread = jnp.mean(center * center, axis=-1, keepdims=True)
        final = center * lax.rsqrt(spread + EPS) * (1.0 + mod(4)) + mod(3)
        predb[0, at, :] = dot_nt(final.astype(jnp.bfloat16), wf[...]).astype(jnp.bfloat16)
        swap(step).start()
        return carry

    lax.fori_loop(0, 4, last_step, 0)

    def guide_step(step, carry):
        at = pl.ds(aligned(step * quarter, quarter), quarter)
        swap(step).wait_recv()
        own = predb[0, at, :].astype(jnp.float32)
        other = predb[1, at, :].astype(jnp.float32)
        cond = jnp.where(half == 0, own, other)
        uncond = jnp.where(half == 0, other, own)
        out[at, :] = uncond + GUIDE * (cond - uncond)
        return carry

    lax.fori_loop(0, 4, guide_step, 0)

    def swap_end(step, carry):
        swap(step).wait_send()
        return carry

    lax.fori_loop(0, 4, swap_end, 0)

    @pl.when(is_spatial)
    def _():
        def end(frame, carry):
            drain(*spatial_send(frame))
            return carry

        lax.fori_loop(0, ROLES, end, 0)

    @pl.when(jnp.logical_not(is_spatial))
    def _():
        def end(frame, carry):
            drain(*temporal_send(frame))
            return carry

        lax.fori_loop(0, n2, end, 0)

    for end in finish:
        end()


def per_device(latent, text_embed, text_mask, modulation, w_in, w_qkv, w_attn_out, w_final):
    count = lax.axis_size("seq")
    positions = latent.shape[1] // CHAN
    depth = w_in.shape[1]
    n2 = count // 2
    members = n2 // ROLES
    width = HEADS * HDIM // ROLES
    cols = w_qkv.shape[1]
    gran = next(g for g in range(min(cols, width), 0, -16) if cols % g == 0 and width % (4 * g) == 0)
    offs, mine = width // gran, cols // gran
    chips = n2 // 2
    rows = ROLES * positions
    words = text_embed.shape[1]
    bf16, f32 = jnp.bfloat16, jnp.float32
    vmem, anywhere = pl.BlockSpec(memory_space=pltpu.VMEM), pl.BlockSpec(memory_space=pl.ANY)
    sem = pltpu.SemaphoreType.DMA
    guided = pl.pallas_call(
        functools.partial(block_kernel, count, gran),
        out_shape=jax.ShapeDtypeStruct((positions, CHAN), f32),
        in_specs=[vmem, anywhere, vmem, vmem, vmem, anywhere, anywhere, vmem],
        out_specs=vmem,
        scratch_shapes=[
            pltpu.VMEM((rows, CHAN), bf16),
            pltpu.VMEM((3, width, depth), bf16),
            pltpu.VMEM((rows, depth), bf16),
            pltpu.VMEM((words, depth), bf16),
            pltpu.VMEM((3, rows + words, width), bf16),
            pltpu.VMEM((rows, width), bf16),
            pltpu.VMEM((depth, HEADS * HDIM), bf16),
            pltpu.VMEM((positions, HEADS * HDIM), bf16),
            pltpu.VMEM((positions, depth), f32),
            pltpu.VMEM((positions, 128), f32),
            pltpu.VMEM((2, positions, CHAN), bf16),
            sem((SROLES + (ROLES - SROLES) * members,)),
            sem((max(n2, ROLES),)),
            sem((mine, 2, members // 2)),
            sem((3 * offs,)),
            sem((3 * offs,)),
            sem((3 * offs,)),
            sem((2, chips)),
            sem((2 * chips,)),
            sem((3, 2 * chips)),
            sem((count, 2)),
            sem((max(n2, ROLES),)),
            sem((SROLES + (ROLES - SROLES) * members,)),
            sem((4,)),
            sem((4,)),
            sem((2,)),
        ],
        compiler_params=pltpu.CompilerParams(
            collective_id=0, has_side_effects=True, vmem_limit_bytes=64000 * 1024
        ),
        name="block",
    )(
        latent.reshape(positions, CHAN), text_embed, text_mask, jnp.transpose(modulation, (1, 0, 2)),
        w_in, w_qkv.T, w_attn_out.T, w_final.T,
    )
    return guided.reshape(1, positions * CHAN)


def solution(mesh):
    in_specs = (
        P(("groups", "seq"), None),
        P("groups", None, None),
        P("groups", None),
        P("groups", None, None),
        P(),
        P(None, "seq"),
        P(None, "seq"),
        P(),
    )
    out_specs = P(("groups", "seq"), None)
    return jax.shard_map(
        per_device, mesh=mesh, in_specs=in_specs, out_specs=out_specs, check_vma=False
    )
```

profile of v0, /device:TPU:4, one launch (start us, length us, event | category | flops | bytes accessed | tf_op | source)
XLA Modules:
  0.0 144.1 jit_solution(16388435440335518297)
XLA Ops:
  0.0 1.3 reduce
  1.3 0.8 reshape.6.lat
  2.0 140.3 %block.1 = f32[512,64]{1,0:T(8,128)} custom-call(bf16[512,64]{1,0:T(8,128)(2,1)} %reshape.6.lat, bf16[2,128,3072]{2,1,0:T(8,128)(2,1)} %text.1, s32[2,128]{1,0:T(2,128)} %mask.1, f32[5,2,3072]{2,1,0:T(2,128)} %bitcast.7, bf16[64,3072]{1,0:T(8,128)(2,1)} %w_in.1, bf16[288,3072]{1,0:T(8,128)(2,1)} %bitcast.4, bf16[192,1536]{1,0:T(8,128)(2,1)} %bitcast.5, ...), custom_call_target="tpu_custom_call" | custom-call | tf_op jit(solution)/shard_map/block/pallas_call | solution.py:539
  142.3 1.8 %reshape.7 = f32[1,32768]{1,0:T(1,128)} reshape(f32[512,64]{1,0:T(8,128)} %block.1) | data formatting | bytes 262144 | tf_op jit(solution)/shard_map/reshape | solution.py:580
where the time goes:
time: 146 us; the launch traced here: 144 us
  Pallas kernels  140 us (96%)
  local copies, waits for them, and re-layouts  2.55 us (2%)
    pallas_call x1, Pallas kernels, per_device(): pl.pallas_call(functools.partial(block_kernel, count, gran), out_shape=ja...  140 us

commit v1 on v0

v1 whole, which is shorter than its diff:
```python
import functools

import jax
import jax.numpy as jnp
from jax import lax
from jax.experimental import pallas as pl
from jax.experimental.pallas import tpu as pltpu
from jax.sharding import PartitionSpec as P

HDIM = 128
SHEADS = 6
THEADS = 6
CHAN = 64
HEADS = 12
ROLES = 4
SROLES = 2
ROLE_OF = ((0, 2, 3, 1), (2, 0, 1, 3))

EPS = 1e-06
GUIDE = 5.0
NT = (((1,), (1,)), ((), ()))


def pick(table, *at):
    if not at:
        return jnp.int32(table)
    picked = pick(table[0], *at[1:])
    for number in range(1, len(table)):
        picked = jnp.where(at[0] == number, pick(table[number], *at[1:]), picked)
    return picked


def dot_nt(a, b):
    return lax.dot_general(a, b, NT, preferred_element_type=jnp.float32)


def normalize(values):
    center = values - jnp.mean(values, axis=-1, keepdims=True)
    spread = jnp.mean(center * center, axis=-1, keepdims=True)
    return center * lax.rsqrt(spread + EPS)


def block_kernel(
    count, gran, lat, text, mask, mods, w_in, wq, wo, wf, out,
    latbuf, w_two, wf_two, wbuf, hbuf, tbuf, pbuf, obuf, wob, jbuf, blk, acc, predb,
    lat_send, lat_recv, w_send, w_xsend, w_tsend, w_recv, wo_send, wo_xsend, wo_tsend, wo_recv,
    j_send, j_recv, p_send, p_recv, loc,
):
    packed = lat.shape[0]
    positions = 2 * packed
    depth = w_in.shape[1]
    n2 = count // 2
    chips = n2 // 2
    team, me = lax.axis_index("groups"), lax.axis_index("seq")
    plane = lax.rem(team, 2)
    half = lax.div(me, n2)
    local = lax.rem(me, n2)
    core = lax.rem(me, 2)
    chip = lax.div(local, 2)
    role = pick(ROLE_OF, half, lax.rem(chip, ROLES))
    seat_of = [[row.index(which) for which in range(ROLES)] for row in ROLE_OF]
    members = n2 // ROLES
    pairs = members // 2
    spot = lax.div(chip, ROLES) * 2 + core
    span = positions // members
    rows = ROLES * positions
    width = wbuf.shape[1]
    heads = width // HDIM
    offs = HDIM // gran
    mine = wq.shape[0] // gran
    is_spatial = role < SROLES

    twin = {"seq": me + 1 - 2 * core}
    across = {"groups": team + 1 - 2 * plane}

    def device(side, which, at):
        return side * n2 + (lax.div(at, 2) * ROLES + pick(seat_of, side, which)) * 2 + lax.rem(at, 2)

    def remote(src, dst, send, recv, peer):
        return pltpu.make_async_remote_copy(
            src_ref=src, dst_ref=dst, send_sem=send, recv_sem=recv,
            device_id=peer, device_id_type=pl.DeviceIdType.MESH,
        )

    finish = []

    def go(src, dst, send, recv, peer):
        remote(src, dst, send, recv, peer).start()
        finish.append(lambda: remote(src, dst, send, recv, peer).wait_send())

    def push(src, dst, send, recv, to):
        def far():
            return remote(src, dst, send, recv, {"seq": to})

        @pl.when(to == me)
        def _():
            pltpu.make_async_copy(src, dst, recv).start()

        @pl.when(to != me)
        def _():
            far().start()

        def end():
            @pl.when(to != me)
            def _():
                far().wait_send()

        finish.append(end)

    def arrived(view, sem):
        pltpu.make_async_copy(view, view, sem).wait()

    def aligned(value, unit):
        return pl.multiple_of(value, unit)

    barrier = pltpu.get_barrier_semaphore()

    def greet(step, carry):
        peer = lax.rem(me + step, count)
        pl.semaphore_signal(barrier, inc=1, device_id={"seq": peer}, device_id_type=pl.DeviceIdType.MESH)
        return carry

    pl.semaphore_signal(barrier, inc=1, device_id=across, device_id_type=pl.DeviceIdType.MESH)
    lax.fori_loop(1, count, greet, 0)

    shard = wo.shape[0]
    unit = shard // (2 * heads)
    own_wo = pltpu.make_async_copy(wo, wob.at[pl.ds(aligned(me * shard, shard), shard)], loc.at[0])
    own_text = pltpu.make_async_copy(text.at[half], tbuf, loc.at[1])
    own_wo.start()
    own_text.start()
    chan = w_in.shape[0]
    none = jnp.zeros((chan, depth), jnp.bfloat16)
    for odd in range(2):
        for two, one in ((w_two, w_in), (wf_two, wf)):
            two[odd, pl.ds(odd * chan, chan), :] = one[...]
            two[odd, pl.ds((1 - odd) * chan, chan), :] = none
    pl.semaphore_wait(barrier, count)

    for which in range(SROLES):
        to = device(half, which, lax.div(local, ROLES))
        slot = lax.rem(local, ROLES)
        push(
            lat, latbuf.at[pl.ds(aligned(slot * packed, packed), packed)],
            lat_send.at[which], lat_recv.at[slot], to,
        )
    for which in range(SROLES, ROLES):
        for at in range(members):
            push(
                lat.at[pl.ds(at * span % packed, span)], latbuf.at[pl.ds(aligned(local * span, span), span)],
                lat_send.at[SROLES + (which - SROLES) * members + at], lat_recv.at[local],
                device(half, which, jnp.int32(at)),
            )

    def slot_view(head, part, off):
        return wbuf.at[head, pl.ds(aligned(part * HDIM + off * gran, gran), gran)]

    def slot_sem(head, part, off):
        return (head * 3 + part) * offs + off

    def crosses(head, part, off):
        column = (part * HEADS + role * heads + head) * HDIM + off * gran
        return lax.div(lax.div(column, wq.shape[0]), n2) != half

    def owner_loop(begin, head_first, head_last):
        def visit(turn, carry):
            wanted, k = lax.div(turn, mine), lax.rem(turn, mine)
            number = me * mine + k
            off = lax.rem(number, offs)
            whole = lax.div(number, offs)
            part, head_at = lax.div(whole, HEADS), lax.rem(whole, HEADS)
            which, head = lax.div(head_at, heads), lax.rem(head_at, heads)
            src = wq.at[pl.ds(aligned(k * gran, gran), gran)]
            dst, recv = slot_view(head, part, off), w_recv.at[slot_sem(head, part, off)]
            turned = lax.rem(lax.div(off, 2), 2) == plane
            for far in (1, 0):
                side = half + far * (1 - 2 * half)
                for pair in range(pairs):
                    to = device(side, which, pair * 2 + lax.rem(off, 2))
                    use = head == wanted
                    if far:
                        use = jnp.logical_and(use, turned)

                    @pl.when(jnp.logical_and(use, to != me))
                    def _(to=to, far=far, pair=pair):
                        copy = remote(src, dst, w_send.at[k, far, pair], recv, {"seq": to})
                        copy.start() if begin else copy.wait_send()

                    if begin and not far:

                        @pl.when(jnp.logical_and(use, to == me))
                        def _():
                            pltpu.make_async_copy(src, dst, recv).start()

            return carry

        lax.fori_loop(head_first * mine, head_last * mine, visit, 0)

    finish.append(lambda: owner_loop(False, 0, heads))

    def wo_view(owner, side, piece):
        if piece == heads - 1:
            return wob.at[pl.ds(aligned(owner * shard + 2 * piece * unit, unit), 2 * unit)]
        return wob.at[pl.ds(aligned(owner * shard + (2 * piece + side) * unit, unit), unit)]

    mirror = me + n2 * (1 - 2 * half)

    def in_half(step):
        return half * n2 + lax.rem(chip + step, chips) * 2 + core

    def in_other(step):
        return (1 - half) * n2 + lax.rem(chip + step, chips) * 2 + core

    def wo_own_sends(piece):
        if piece == heads - 1:
            src = wo.at[pl.ds(2 * piece * unit, 2 * unit)]
        else:
            src = wo.at[pl.ds(aligned((2 * piece + plane) * unit, unit), unit)]
        dst, recv = wo_view(me, plane, piece), wo_recv.at[piece, me, 0]
        go(src, dst, wo_send.at[piece, 0, 0], recv, {"seq": mirror})
        for step in range(1, chips):
            go(src, dst, wo_send.at[piece, 0, step], recv, {"seq": in_half(step)})

    def wo_spread(owner, number, piece):
        view = wo_view(owner, plane, piece)
        if piece < heads - 1:
            go(view, view, wo_xsend.at[piece, number], wo_recv.at[piece, owner, 1], across)
        go(view, view, wo_tsend.at[piece, 0, number], wo_recv.at[piece, owner, 0], twin)

    def wo_take(owner, number, piece):
        arrived(wo_view(owner, plane, piece), wo_recv.at[piece, owner, 0])
        wo_spread(owner, number, piece)

    others = [(in_half(step), step) for step in range(1, chips)]
    far_others = [(in_other(step), chips + step) for step in range(1, chips)]

    def wo_near_take(piece):
        for owner, number in others:
            wo_take(owner, number, piece)

    def wo_mirror(piece):
        view = wo_view(mirror, plane, piece)
        arrived(view, wo_recv.at[piece, mirror, 0])
        for step in range(1, chips):
            go(
                view, view, wo_send.at[piece, 1, step], wo_recv.at[piece, mirror, 0],
                {"seq": in_half(step)},
            )
        wo_spread(mirror, 0, piece)

    def wo_far_take(piece):
        for owner, number in far_others:
            wo_take(owner, number, piece)

    def wo_cross_take(piece, owners):
        for owner, number in owners:
            view = wo_view(owner, 1 - plane, piece)
            arrived(view, wo_recv.at[piece, owner, 1])
            go(view, view, wo_tsend.at[piece, 1, number], wo_recv.at[piece, owner, 1], twin)

    def wo_wait(owners):
        for piece in range(heads):
            for owner, _ in owners:
                owner = owner + 1 - 2 * core
                arrived(wo_view(owner, plane, piece), wo_recv.at[piece, owner, 0])
                if piece < heads - 1:
                    arrived(wo_view(owner, 1 - plane, piece), wo_recv.at[piece, owner, 1])

    def wo_own_wait():
        own_wo.wait()
        other = me + 1 - 2 * core
        arrived(wob.at[pl.ds(aligned(other * shard, shard), shard)], wo_recv.at[0, other, 0])

    far_owners = [(mirror, 0)] + far_others

    own_rows = wob.at[pl.ds(aligned(me * shard, shard), shard)]
    go(wo, own_rows, wo_tsend.at[0, 0, chips], wo_recv.at[0, me, 0], twin)
    for piece in range(heads):
        owner_loop(True, piece, piece + 1)
        wo_own_sends(piece)

    def mod(which):
        return jnp.where(half == 0, mods[which, 0:1, :], mods[which, 1:2, :])

    tall = min(128, span)
    blocks = packed // tall

    def start_step(step, carry):
        src = pl.ds(aligned(lax.rem(step, blocks) * tall, tall), tall)
        blk[pl.ds(aligned(step * tall, tall), tall), :] = jnp.dot(
            lat[src, :], w_two[lax.div(step, blocks)], preferred_element_type=jnp.float32
        )
        return carry

    lax.fori_loop(0, 2 * blocks, start_step, 0)

    @pl.when(is_spatial)
    def _():
        for slot in range(ROLES):
            arrived(latbuf.at[pl.ds(slot * packed, packed)], lat_recv.at[slot])

    @pl.when(jnp.logical_not(is_spatial))
    def _():
        for frame in range(n2):
            arrived(latbuf.at[pl.ds(frame * span, span)], lat_recv.at[frame])

    odd_span = lax.div(spot * span, packed)

    def hidden_step(step, carry):
        at = pl.ds(aligned(step * tall, tall), tall)
        frame, inner = lax.div(step, 2 * blocks), lax.rem(step, 2 * blocks)
        from_block = jnp.where(is_spatial, frame * blocks + lax.rem(inner, blocks), step)
        odd = jnp.where(is_spatial, lax.div(inner, blocks), odd_span)
        src = pl.ds(aligned(from_block * tall, tall), tall)
        begun = jnp.dot(latbuf[src, :], w_two[odd], preferred_element_type=jnp.float32)
        hbuf[at, :] = (normalize(begun) * (1.0 + mod(1)) + mod(0)).astype(jnp.bfloat16)
        return carry

    lax.fori_loop(0, rows // tall, hidden_step, 0)
    own_text.wait()

    def relay(head, part, off, over):
        view, number = slot_view(head, part, off), slot_sem(head, part, off)
        arrived(view, w_recv.at[number])
        if over:
            remote(view, view, w_xsend.at[number], w_recv.at[number], across).start()
        remote(view, view, w_tsend.at[number], w_recv.at[number], twin).start()

    groups = [(part, e) for part in range(3) for e in range(offs // 4)]

    def take_crossing(head):
        for part, e in groups:
            off = core + 2 * plane + 4 * e

            @pl.when(crosses(head, part, off))
            def _(part=part, off=off):
                relay(head, part, off, True)

    def take_near(head):
        for part, e in groups:
            off = core + 2 * plane + 4 * e

            @pl.when(jnp.logical_not(crosses(head, part, off)))
            def _(part=part, off=off):
                relay(head, part, off, False)

    def take_rest(head):
        for part, e in groups:
            relay(head, part, core + 2 * (1 - plane) + 4 * e, False)

    def take_twin(head):
        for part, e in groups:
            for side in range(2):
                off = 1 - core + 2 * side + 4 * e
                arrived(slot_view(head, part, off), w_recv.at[slot_sem(head, part, off)])

    def relay_end():
        for head in range(heads):
            for part, e in groups:
                off = core + 2 * plane + 4 * e
                view, number = slot_view(head, part, off), slot_sem(head, part, off)

                @pl.when(crosses(head, part, off))
                def _(view=view, number=number):
                    remote(view, view, w_xsend.at[number], w_recv.at[number], across).wait_send()

                for off in (core + 2 * plane + 4 * e, core + 2 * (1 - plane) + 4 * e):
                    view, number = slot_view(head, part, off), slot_sem(head, part, off)
                    remote(view, view, w_tsend.at[number], w_recv.at[number], twin).wait_send()

    finish.append(relay_end)

    words = tbuf.shape[0]

    def project(head, between=None):
        def body(turn, carry):
            at = pl.ds(aligned(turn * positions, positions), positions)
            pbuf[head, at, :] = dot_nt(hbuf[at, :], wbuf[head]).astype(jnp.bfloat16)
            return carry

        if between is None:
            lax.fori_loop(0, ROLES, body, 0)
        else:
            lax.fori_loop(0, ROLES // 2, body, 0)
            between()
            lax.fori_loop(ROLES // 2, ROLES, body, 0)

        @pl.when(is_spatial)
        def _():
            pbuf[head, pl.ds(rows, words), :] = dot_nt(tbuf[...], wbuf[head]).astype(jnp.bfloat16)

    scale = HDIM ** (-0.5)
    query_at, keys_at, vals_at = (pl.ds(part * HDIM, HDIM) for part in range(3))

    def lanes(head):
        return pl.ds(aligned((role * heads + head) * HDIM, HDIM), HDIM)

    def spatial_send(head, frame):
        to = half * n2 + spot * ROLES + frame
        src = obuf.at[head, pl.ds(aligned(frame * positions, positions), positions)]
        return (src, jbuf.at[:, lanes(head)], j_send.at[head, frame], j_recv.at[head, role]), to

    def temporal_send(head, frame):
        to = half * n2 + frame
        src = obuf.at[head, pl.ds(aligned(frame * span, span), span)]
        dst = jbuf.at[pl.ds(aligned(spot * span, span), span), lanes(head)]
        recv = j_recv.at[head, SROLES + (role - SROLES) * members + spot]
        return (src, dst, j_send.at[head, frame], recv), to

    def dispatch(refs, to):
        src, dst, send, recv = refs

        @pl.when(to == me)
        def _():
            pltpu.make_async_copy(src, dst, recv).start()

        @pl.when(to != me)
        def _():
            remote(src, dst, send, recv, {"seq": to}).start()

    def drain(refs, to):
        @pl.when(to != me)
        def _():
            remote(*refs, {"seq": to}).wait_send()

    def attend_spatial(head):
        live = jnp.where(half == 0, mask[0:1, :], mask[1:2, :]) > 0
        tallq = positions // 2

        def frame_step(frame, carry):
            base = frame * positions
            at = pl.ds(aligned(base, positions), positions)
            keys, vals = pbuf[head, at, keys_at], pbuf[head, at, vals_at]
            tkeys, tvals = pbuf[head, pl.ds(rows, words), keys_at], pbuf[head, pl.ds(rows, words), vals_at]
            for piece in range(2):
                here = pl.ds(aligned(base + piece * tallq, tallq), tallq)
                query = pbuf[head, here, query_at]
                near = dot_nt(query, keys) * scale
                side = jnp.where(live, dot_nt(query, tkeys) * scale, -1e30)
                top = jnp.maximum(
                    jnp.max(near, axis=-1, keepdims=True), jnp.max(side, axis=-1, keepdims=True)
                )
                near = jnp.exp(near - top)
                side = jnp.exp(side - top)
                total = jnp.sum(near, axis=-1, keepdims=True) + jnp.sum(side, axis=-1, keepdims=True)
                mixed = jnp.dot(
                    near.astype(jnp.bfloat16), vals, preferred_element_type=jnp.float32
                ) + jnp.dot(side.astype(jnp.bfloat16), tvals, preferred_element_type=jnp.float32)
                obuf[head, here, :] = (mixed / total).astype(jnp.bfloat16)
            dispatch(*spatial_send(head, frame))
            return carry

        lax.fori_loop(0, ROLES, frame_step, 0)

    def attend_temporal(head):
        few = 256 // n2
        size = few * n2
        row_at = lax.rem(lax.broadcasted_iota(jnp.int32, (size, size), 0), few)
        col_at = lax.rem(lax.broadcasted_iota(jnp.int32, (size, size), 1), few)
        same = row_at == col_at

        def place_step(place, carry):
            def at(frame):
                return pl.ds(aligned(frame * span + place * few, few), few)

            query, keys, vals = (
                jnp.concatenate([pbuf[head, at(frame), cols] for frame in range(n2)], axis=0)
                for cols in (query_at, keys_at, vals_at)
            )
            scores = jnp.where(same, dot_nt(query, keys) * scale, -1e30)
            weights = jnp.exp(scores - jnp.max(scores, axis=-1, keepdims=True))
            total = jnp.sum(weights, axis=-1, keepdims=True)
            mixed = jnp.dot(weights.astype(jnp.bfloat16), vals, preferred_element_type=jnp.float32)
            mixed = (mixed / total).astype(jnp.bfloat16)
            for frame in range(n2):
                obuf[head, at(frame), :] = mixed[frame * few : (frame + 1) * few]
            return carry

        lax.fori_loop(0, span // few, place_step, 0)

        def send_step(frame, carry):
            dispatch(*temporal_send(head, frame))
            return carry

        lax.fori_loop(0, n2, send_step, 0)

    def attend(head):
        @pl.when(is_spatial)
        def _():
            attend_spatial(head)

        @pl.when(jnp.logical_not(is_spatial))
        def _():
            attend_temporal(head)

    take_crossing(0)
    take_near(0)
    take_rest(0)
    take_twin(0)
    project(0, lambda: take_crossing(1))
    wo_near_take(0)
    wo_mirror(0)
    attend(0)
    take_near(1)
    take_crossing(2)
    take_rest(1)
    take_twin(1)
    project(1, lambda: wo_far_take(0))
    wo_near_take(1)
    wo_mirror(1)
    attend(1)
    wo_cross_take(0, others + far_owners)
    take_near(2)
    take_rest(2)
    take_twin(2)
    wo_mirror(2)
    project(2, lambda: wo_far_take(1))
    attend(2)
    wo_near_take(2)
    wo_cross_take(1, others)
    wo_own_wait()
    wo_wait(others)

    acc[...] = jnp.zeros_like(acc)
    strip = depth // 6

    for head in range(heads):
        for which in range(SROLES):
            lane = pl.ds((which * heads + head) * HDIM, HDIM)
            arrived(jbuf.at[:, lane], j_recv.at[head, which])
        for which in range(SROLES, ROLES):
            lane = pl.ds((which * heads + head) * HDIM, HDIM)
            for at in range(members):
                arrived(
                    jbuf.at[pl.ds(at * span, span), lane],
                    j_recv.at[head, SROLES + (which - SROLES) * members + at],
                )

    def mix_step(step, carry):
        cols = pl.ds(aligned(step * strip, strip), strip)
        gate = jnp.where(half == 0, mods[2, 0:1, cols], mods[2, 1:2, cols])
        value = blk[:, cols] + gate * dot_nt(jbuf[...], wob[cols, :])
        blk[:, cols] = value
        part = value[:, :128]
        for piece in range(1, strip // 128):
            part = part + value[:, piece * 128 : (piece + 1) * 128]
        acc[...] += part
        return carry

    lax.fori_loop(3 * half, 3 * half + 3, mix_step, 0)
    wo_far_take(2)
    wo_cross_take(1, far_owners)
    wo_wait(far_owners)
    lax.fori_loop(3 - 3 * half, 6 - 3 * half, mix_step, 0)

    steps = 4
    low = packed // steps

    def swap(step):
        at = pl.ds(aligned(step * low, low), low)
        return remote(
            predb.at[0, at], predb.at[1, at], p_send.at[step], p_recv.at[step], {"seq": mirror}
        )

    def last_step(step, carry):
        pred = None
        for odd in range(2):
            at = pl.ds(aligned(odd * packed + step * low, low), low)
            mean = jnp.sum(acc[at, :], axis=-1, keepdims=True) / depth
            center = blk[at, :] - mean
            spread = jnp.mean(center * center, axis=-1, keepdims=True)
            final = center * lax.rsqrt(spread + EPS) * (1.0 + mod(4)) + mod(3)
            here = dot_nt(final.astype(jnp.bfloat16), wf_two[odd])
            pred = here if pred is None else pred + here
        predb[0, pl.ds(aligned(step * low, low), low), :] = pred.astype(jnp.bfloat16)
        swap(step).start()
        return carry

    lax.fori_loop(0, steps, last_step, 0)

    def guide_step(step, carry):
        at = pl.ds(aligned(step * low, low), low)
        swap(step).wait_recv()
        own = predb[0, at, :].astype(jnp.float32)
        other = predb[1, at, :].astype(jnp.float32)
        cond = jnp.where(half == 0, own, other)
        uncond = jnp.where(half == 0, other, own)
        out[at, :] = uncond + GUIDE * (cond - uncond)
        return carry

    lax.fori_loop(0, steps, guide_step, 0)

    def swap_end(step, carry):
        swap(step).wait_send()
        return carry

    lax.fori_loop(0, steps, swap_end, 0)

    for head in range(heads):

        @pl.when(is_spatial)
        def _(head=head):
            def end(frame, carry):
                drain(*spatial_send(head, frame))
                return carry

            lax.fori_loop(0, ROLES, end, 0)

        @pl.when(jnp.logical_not(is_spatial))
        def _(head=head):
            def end(frame, carry):
                drain(*temporal_send(head, frame))
                return carry

            lax.fori_loop(0, n2, end, 0)

    for end in finish:
        end()


def per_device(latent, text_embed, text_mask, modulation, w_in, w_qkv, w_attn_out, w_final):
    count = lax.axis_size("seq")
    positions = latent.shape[1] // CHAN
    depth = w_in.shape[1]
    n2 = count // 2
    members = n2 // ROLES
    width = HEADS * HDIM // ROLES
    cols = w_qkv.shape[1]
    gran = next(g for g in range(HDIM // 4, 0, -16) if cols % g == 0 and HDIM % (4 * g) == 0)
    heads = width // HDIM
    offs, mine = HDIM // gran, cols // gran
    chips = n2 // 2
    rows = ROLES * positions
    words = text_embed.shape[1]
    bf16, f32 = jnp.bfloat16, jnp.float32
    vmem, anywhere = pl.BlockSpec(memory_space=pltpu.VMEM), pl.BlockSpec(memory_space=pl.ANY)
    sem = pltpu.SemaphoreType.DMA
    guided = pl.pallas_call(
        functools.partial(block_kernel, count, gran),
        out_shape=jax.ShapeDtypeStruct((positions // 2, 2 * CHAN), f32),
        in_specs=[vmem, anywhere, vmem, vmem, vmem, anywhere, anywhere, vmem],
        out_specs=vmem,
        scratch_shapes=[
            pltpu.VMEM((rows, 2 * CHAN), bf16),
            pltpu.VMEM((2, 2 * CHAN, depth), bf16),
            pltpu.VMEM((2, 2 * CHAN, depth), bf16),
            pltpu.VMEM((3, width, depth), bf16),
            pltpu.VMEM((rows, depth), bf16),
            pltpu.VMEM((words, depth), bf16),
            pltpu.VMEM((3, rows + words, width), bf16),
            pltpu.VMEM((heads, rows, HDIM), bf16),
            pltpu.VMEM((depth, HEADS * HDIM), bf16),
            pltpu.VMEM((positions, HEADS * HDIM), bf16),
            pltpu.VMEM((positions, depth), f32),
            pltpu.VMEM((positions, 128), f32),
            pltpu.VMEM((2, positions // 2, 2 * CHAN), bf16),
            sem((SROLES + (ROLES - SROLES) * members,)),
            sem((max(n2, ROLES),)),
            sem((mine, 2, members // 2)),
            sem((heads * 3 * offs,)),
            sem((heads * 3 * offs,)),
            sem((heads * 3 * offs,)),
            sem((heads, 2, chips)),
            sem((heads, 2 * chips)),
            sem((heads, 2, 2 * chips)),
            sem((heads, count, 2)),
            sem((heads, max(n2, ROLES))),
            sem((heads, SROLES + (ROLES - SROLES) * members)),
            sem((4,)),
            sem((4,)),
            sem((2,)),
        ],
        compiler_params=pltpu.CompilerParams(
            collective_id=0, has_side_effects=True, vmem_limit_bytes=64000 * 1024
        ),
        name="block",
    )(
        latent.reshape(positions // 2, 2 * CHAN), text_embed, text_mask, jnp.transpose(modulation, (1, 0, 2)),
        w_in, w_qkv.T, w_attn_out.T, w_final.T,
    )
    return guided.reshape(1, positions * CHAN)


def solution(mesh):
    in_specs = (
        P(("groups", "seq"), None),
        P("groups", None, None),
        P("groups", None),
        P("groups", None, None),
        P(),
        P(None, "seq"),
        P(None, "seq"),
        P(),
    )
    out_specs = P(("groups", "seq"), None)
    return jax.shard_map(
        per_device, mesh=mesh, in_specs=in_specs, out_specs=out_specs, check_vma=False
    )
```

time: 146 us -> 133 us (0.911)
  Pallas kernels: 140 us -> 127 us
    pallas_call x1, Pallas kernels: 140 us -> 127 us  [per_device(): pl.pallas_call(functools.partial(block_kernel, count, gran), out_shape=ja...]
    reshape x2 -> x0, local copies, waits for them, and re-layouts: 2.55 us -> none  [the longest x1 1.79 us: per_device(): return guided.reshape(1, positions * CHAN)]
    unnamed x0 -> x1, local copies, waits for them, and re-layouts: none -> 1.57 us
where the time goes in v1:
time: 133 us; the launch traced here: 130 us
  Pallas kernels  127 us (95%)
  other arithmetic  1.89 us (1%)
  local copies, waits for them, and re-layouts  1.57 us (1%)
    pallas_call x1, Pallas kernels, per_device(): pl.pallas_call(functools.partial(block_kernel, count, gran), out_shape=ja...  127 us

profile of v1, /device:TPU:4, one launch (start us, length us, event | category | flops | bytes accessed | tf_op | source)
XLA Modules:
  0.0 130.4 jit_solution(5920099312163940585)
XLA Ops:
  0.0 1.9 %reduce = bf16[32768]{0:T(1024)(128)(2,1)} reduce(bf16[1,32768]{1,0:T(2,128)(2,1)} %param.8, bf16[]{:T(256)} %constant.1), dimensions={0}, to_apply=%param.8.reduce_sub_computation | reduce | bytes 131074 | tf_op args[0]
  1.9 126.9 %block.1 = f32[256,128]{1,0:T(8,128)} custom-call(bf16[256,128]{1,0:T(8,128)(2,1)} %bitcast.10, bf16[2,128,3072]{2,1,0:T(8,128)(2,1)} %text.1, s32[2,128]{1,0:T(2,128)} %mask.1, f32[5,2,3072]{2,1,0:T(2,128)} %bitcast.11, bf16[64,3072]{1,0:T(8,128)(2,1)} %w_in.1, bf16[288,3072]{1,0:T(8,128)(2,1)} %bitcast.6, bf16[192,1536]{1,0:T(8,128)(2,1)} %bitcast.7, ...), custom_call_target="tpu_custom_call" | custom-call | tf_op jit(solution)/shard_map/block/pallas_call | solution.py:638
  128.8 1.6 %copy.10 = f32[1,32768]{1,0:T(1,128)} copy(f32[1,32768]{1,0:T(1,128)} %bitcast.8) | data formatting | bytes 262144

commit v2 on v1

--- a/solution.py
+++ b/solution.py
@@ -160,7 +160,7 @@
 
     def crosses(head, part, off):
         column = (part * HEADS + role * heads + head) * HDIM + off * gran
-        return lax.div(lax.div(column, wq.shape[0]), n2) != half
+        return lax.div(column, 2 * wq.shape[0]) != lax.div(me, 2)
 
     def owner_loop(begin, head_first, head_last):
         def visit(turn, carry):
@@ -177,9 +177,8 @@
                 side = half + far * (1 - 2 * half)
                 for pair in range(pairs):
                     to = device(side, which, pair * 2 + lax.rem(off, 2))
-                    use = head == wanted
-                    if far:
-                        use = jnp.logical_and(use, turned)
+                    stays = lax.div(to, 2) == lax.div(me, 2)
+                    use = jnp.logical_and(head == wanted, jnp.logical_or(turned, stays))
 
                     @pl.when(jnp.logical_and(use, to != me))
                     def _(to=to, far=far, pair=pair):
@@ -316,7 +315,6 @@
         hbuf[at, :] = (normalize(begun) * (1.0 + mod(1)) + mod(0)).astype(jnp.bfloat16)
         return carry
 
-    lax.fori_loop(0, rows // tall, hidden_step, 0)
     own_text.wait()
 
     def relay(head, part, off, over):
@@ -493,7 +491,9 @@
         def _():
             attend_temporal(head)
 
+    lax.fori_loop(0, 3 * (rows // tall) // 4, hidden_step, 0)
     take_crossing(0)
+    lax.fori_loop(3 * (rows // tall) // 4, rows // tall, hidden_step, 0)
     take_near(0)
     take_rest(0)
     take_twin(0)
@@ -502,10 +502,10 @@
     wo_mirror(0)
     attend(0)
     take_near(1)
-    take_crossing(2)
     take_rest(1)
     take_twin(1)
-    project(1, lambda: wo_far_take(0))
+    project(1, lambda: take_crossing(2))
+    wo_far_take(0)
     wo_near_take(1)
     wo_mirror(1)
     attend(1)

time: 133 us -> 128 us (0.962)
  Pallas kernels: 127 us -> 123 us
    pallas_call x1, Pallas kernels: 127 us -> 123 us  [per_device(): pl.pallas_call(functools.partial(block_kernel, count, gran), out_shape=ja...]
where the time goes in v2:
time: 128 us; the launch traced here: 126 us
  Pallas kernels  123 us (96%)
  other arithmetic  1.89 us (1%)
  local copies, waits for them, and re-layouts  1.57 us (1%)
    pallas_call x1, Pallas kernels, per_device(): pl.pallas_call(functools.partial(block_kernel, count, gran), out_shape=ja...  123 us

profile of v2, /device:TPU:4, one launch (start us, length us, event | category | flops | bytes accessed | tf_op | source)
XLA Modules:
  0.0 126.2 jit_solution(8703664911253470359)
XLA Ops:
  0.0 1.9 %reduce = bf16[32768]{0:T(1024)(128)(2,1)} reduce(bf16[1,32768]{1,0:T(2,128)(2,1)} %param.8, bf16[]{:T(256)} %constant.1), dimensions={0}, to_apply=%param.8.reduce_sub_computation | reduce | bytes 131074 | tf_op args[0]
  1.9 122.8 %block.1 = f32[256,128]{1,0:T(8,128)} custom-call(bf16[256,128]{1,0:T(8,128)(2,1)} %bitcast.10, bf16[2,128,3072]{2,1,0:T(8,128)(2,1)} %text.1, s32[2,128]{1,0:T(2,128)} %mask.1, f32[5,2,3072]{2,1,0:T(2,128)} %bitcast.11, bf16[64,3072]{1,0:T(8,128)(2,1)} %w_in.1, bf16[288,3072]{1,0:T(8,128)(2,1)} %bitcast.6, bf16[192,1536]{1,0:T(8,128)(2,1)} %bitcast.7, ...), custom_call_target="tpu_custom_call" | custom-call | tf_op jit(solution)/shard_map/block/pallas_call | solution.py:638
  124.7 1.6 %copy.10 = f32[1,32768]{1,0:T(1,128)} copy(f32[1,32768]{1,0:T(1,128)} %bitcast.8) | data formatting | bytes 262144

commit v3 on v2

--- a/solution.py
+++ b/solution.py
@@ -505,11 +505,10 @@
     take_rest(1)
     take_twin(1)
     project(1, lambda: take_crossing(2))
-    wo_far_take(0)
     wo_near_take(1)
     wo_mirror(1)
     attend(1)
-    wo_cross_take(0, others + far_owners)
+    wo_far_take(0)
     take_near(2)
     take_rest(2)
     take_twin(2)
@@ -517,6 +516,7 @@
     project(2, lambda: wo_far_take(1))
     attend(2)
     wo_near_take(2)
+    wo_cross_take(0, others + far_owners)
     wo_cross_take(1, others)
     wo_own_wait()
     wo_wait(others)

time: 128 us -> 124 us (0.969); the launches traced: 126 us -> 124 us
  Pallas kernels: 123 us -> 120 us
    pallas_call x1, Pallas kernels: 123 us -> 120 us  [per_device(): pl.pallas_call(functools.partial(block_kernel, count, gran), out_shape=ja...]
where the time goes in v3:
time: 124 us
  Pallas kernels  120 us (97%)
  other arithmetic  1.89 us (2%)
  local copies, waits for them, and re-layouts  1.57 us (1%)
    pallas_call x1, Pallas kernels, per_device(): pl.pallas_call(functools.partial(block_kernel, count, gran), out_shape=ja...  120 us

profile of v3, /device:TPU:4, one launch (start us, length us, event | category | flops | bytes accessed | tf_op | source)
XLA Modules:
  0.0 123.7 jit_solution(18362247110587890052)
XLA Ops:
  0.0 1.9 %reduce = bf16[32768]{0:T(1024)(128)(2,1)} reduce(bf16[1,32768]{1,0:T(2,128)(2,1)} %param.8, bf16[]{:T(256)} %constant.1), dimensions={0}, to_apply=%param.8.reduce_sub_computation | reduce | bytes 131074 | tf_op args[0]
  1.9 120.2 %block.1 = f32[256,128]{1,0:T(8,128)} custom-call(bf16[256,128]{1,0:T(8,128)(2,1)} %bitcast.10, bf16[2,128,3072]{2,1,0:T(8,128)(2,1)} %text.1, s32[2,128]{1,0:T(2,128)} %mask.1, f32[5,2,3072]{2,1,0:T(2,128)} %bitcast.11, bf16[64,3072]{1,0:T(8,128)(2,1)} %w_in.1, bf16[288,3072]{1,0:T(8,128)(2,1)} %bitcast.6, bf16[192,1536]{1,0:T(8,128)(2,1)} %bitcast.7, ...), custom_call_target="tpu_custom_call" | custom-call | tf_op jit(solution)/shard_map/block/pallas_call | solution.py:638
  122.1 1.6 %copy.10 = f32[1,32768]{1,0:T(1,128)} copy(f32[1,32768]{1,0:T(1,128)} %bitcast.8) | data formatting | bytes 262144
